TPU v7x, 256 devices: a whole 4x4x8 slice. The times are simulated.
256 devices in a mesh: seq: 32 (over z_hi, x, core), head: 8 (over y, z_lo).
Axes of the slice: x: 4, y: 4, z: 8 (z_hi: 4, z_lo: 2; z = z_hi * 2 + z_lo), core: 2. Of those that a mesh axis runs over, the one named last changes fastest.
Arguments:
- tokens: bfloat16 [4096, 3072], P('seq', 'head'), may hold values from -5 to 5, as said below
- norm_gains: float32 [5, 3072], replicated, may hold values from 0.25 to 1.75
- window: int32 [24], P('head'), may hold values from 16 to 128, as said below
- self_query: bfloat16 [3072, 3072], P(None, 'head')
- self_key_value: bfloat16 [2, 3072, 1024], P(None, None, 'head')
- self_output: bfloat16 [3072, 3072], P('head'), may hold values from -0.4375 to 0.4375
- shared_key_value: bfloat16 [2, 3072, 1024], P(None, None, 'head')
- cross_query: bfloat16 [3, 3072, 3072], P(None, 'seq', 'head')
- cross_output: bfloat16 [3, 3072, 3072], P(None, 'head', 'seq'), may hold values from -0.4375 to 0.4375
- key_blocks: int32 [3, 32, 16], P(None, 'seq'), may hold values from -1 to 31, as said below
Outputs:
- mixed: float32 [4096, 3072], P('seq', 'head')
Inputs may be any that keep to these rules, and one draw needn't show every extreme that they name: `tokens`: rows may hold near twins of the rows beside them. Some head has a window of exactly 128 and some head one of exactly 16. `key_blocks`: the row of query block b lists distinct blocks at or before b, the first being b itself; it holds min(16, b + 1) blocks and -1 in the remaining slots.
All inputs are finite; a program needn't handle non-finite values.
Results may differ from a plain program's by a relative error of at most 0.04.
Values may be sent and summed in bfloat16 or wider, within the bound.
A program may use at most 64 MiB of HBM per device.

v0:
```python
import jax
import jax.numpy as jnp
from jax import lax
from jax.sharding import PartitionSpec as P

HEAD_WIDTH = 128
KEY_BLOCK_TOKENS = 128
LISTED_BLOCKS = 16
SECTIONS = 3
EPSILON = 1e-06
MASKED = -1e30


def passed_along(value, axis, steps):
    count = lax.axis_size(axis)
    initial, last = (max(0, -steps), min(count, count - steps))
    return lax.ppermute(value, axis, [(source, source + steps) for source in range(initial, last)])


def softmax_rows(scores, allowed):
    scores = jnp.where(allowed, scores, MASKED)
    largest = jnp.max(scores, axis=-1, keepdims=True)
    weights = jnp.exp(scores - largest)
    return (weights / jnp.sum(weights, axis=-1, keepdims=True)).astype(jnp.bfloat16)


def body(
    tokens,
    norm_gains,
    window,
    self_query,
    self_key_value,
    self_output,
    shared_key_value,
    cross_query,
    cross_output,
    key_blocks,
):
    seq_rank = lax.axis_index("seq")
    row_count, local_width = tokens.shape
    kv_columns = self_key_value.shape[2]
    query_columns = self_query.shape[1]
    kv_heads = kv_columns // HEAD_WIDTH
    query_group_width = query_columns // kv_columns
    scale_factor = HEAD_WIDTH ** (-0.5)

    def normed_full(stream, gain_row):
        gathered = lax.all_gather(
            stream.astype(jnp.float32).astype(jnp.bfloat16), "head", axis=1, tiled=True
        ).astype(jnp.float32)
        factor = lax.rsqrt(jnp.mean(gathered * gathered, axis=1, keepdims=True) + EPSILON)
        return (gathered * factor * gain_row[None, :]).astype(jnp.bfloat16)

    def add_branch(stream, partial_value):
        summed = lax.psum_scatter(
            partial_value.astype(jnp.bfloat16), "head", scatter_dimension=1, tiled=True
        ).astype(jnp.float32)
        return stream.astype(jnp.float32) + summed

    def project(inputs, weight):
        return jnp.dot(inputs, weight, preferred_element_type=jnp.float32).astype(jnp.bfloat16)

    first = normed_full(tokens, norm_gains[0])
    query_matrix = project(first, self_query)
    keys_own = project(first, self_key_value[0])
    values_own = project(first, self_key_value[1])
    keys_prev, values_prev = passed_along((keys_own, values_own), "seq", 1)
    near_keys = jnp.concatenate([keys_prev, keys_own], axis=0).reshape(
        2 * row_count, kv_heads, HEAD_WIDTH
    )
    near_values = jnp.concatenate([values_prev, values_own], axis=0).reshape(
        2 * row_count, kv_heads, HEAD_WIDTH
    )
    query_heads = query_matrix.reshape(row_count, kv_heads, query_group_width, HEAD_WIDTH)
    scores = (
        jnp.einsum("tkgd,skd->kgts", query_heads, near_keys, preferred_element_type=jnp.float32)
        * scale_factor
    )
    offsets = (
        jnp.arange(row_count, dtype=jnp.int32)[:, None]
        + row_count
        - jnp.arange(2 * row_count, dtype=jnp.int32)[None, :]
    )
    key_pos = seq_rank * row_count - row_count + jnp.arange(2 * row_count, dtype=jnp.int32)
    window_bounds = window.reshape(kv_heads, query_group_width)
    allowed = (
        (offsets >= 0)[None, None]
        & (offsets[None, None] < window_bounds[:, :, None, None])
        & (key_pos >= 0)[None, None, None, :]
    )
    probs = softmax_rows(scores, allowed)
    context = jnp.einsum("kgts,skd->tkgd", probs, near_values, preferred_element_type=jnp.float32)
    context = context.astype(jnp.bfloat16).reshape(row_count, query_columns)
    stream = add_branch(tokens, jnp.dot(context, self_output, preferred_element_type=jnp.float32))
    cache_in = normed_full(stream, norm_gains[1])
    cached_key_rows = project(cache_in, shared_key_value[0])
    cached_value_rows = project(cache_in, shared_key_value[1])
    all_keys, all_values = (
        lax.all_gather(cached_key_rows, "seq", axis=0, tiled=True),
        lax.all_gather(cached_value_rows, "seq", axis=0, tiled=True),
    )
    key_lookup_matrix = all_keys.reshape(-1, KEY_BLOCK_TOKENS, kv_columns)
    value_lookup_matrix = all_values.reshape(-1, KEY_BLOCK_TOKENS, kv_columns)
    query_blocks = row_count // KEY_BLOCK_TOKENS
    inner = jnp.arange(KEY_BLOCK_TOKENS, dtype=jnp.int32)
    block_ids = seq_rank * query_blocks + jnp.arange(query_blocks, dtype=jnp.int32)
    query_pos = block_ids[:, None] * KEY_BLOCK_TOKENS + inner[None, :]
    for section in range(SECTIONS):
        section_in = normed_full(stream, norm_gains[2 + section])
        query_matrix = jnp.dot(
            section_in,
            lax.all_gather(cross_query[section], "seq", axis=0, tiled=True),
            preferred_element_type=jnp.float32,
        ).astype(jnp.bfloat16)
        lists = key_blocks[section]
        clamped_index = jnp.maximum(lists, 0)
        picked_keys = jnp.take(key_lookup_matrix, clamped_index.reshape(-1), axis=0).reshape(
            query_blocks, LISTED_BLOCKS * KEY_BLOCK_TOKENS, kv_heads, HEAD_WIDTH
        )
        picked_values = jnp.take(value_lookup_matrix, clamped_index.reshape(-1), axis=0).reshape(
            query_blocks, LISTED_BLOCKS * KEY_BLOCK_TOKENS, kv_heads, HEAD_WIDTH
        )
        query_heads = query_matrix.reshape(
            query_blocks, KEY_BLOCK_TOKENS, kv_heads, query_group_width, HEAD_WIDTH
        )
        scores = (
            jnp.einsum(
                "btkgd,bskd->bkgts", query_heads, picked_keys, preferred_element_type=jnp.float32
            )
            * scale_factor
        )
        listed_pos = (clamped_index[:, :, None] * KEY_BLOCK_TOKENS + inner[None, None, :]).reshape(
            query_blocks, LISTED_BLOCKS * KEY_BLOCK_TOKENS
        )
        present = jnp.repeat(lists >= 0, KEY_BLOCK_TOKENS, axis=1)
        allowed = present[:, None, :] & (listed_pos[:, None, :] <= query_pos[:, :, None])
        probs = softmax_rows(scores, allowed[:, None, None])
        context = jnp.einsum(
            "bkgts,bskd->btkgd", probs, picked_values, preferred_element_type=jnp.float32
        )
        context = context.astype(jnp.bfloat16).reshape(row_count, query_columns)
        partial_value = jnp.dot(
            context,
            lax.all_gather(cross_output[section], "seq", axis=1, tiled=True),
            preferred_element_type=jnp.float32,
        )
        stream = add_branch(stream, partial_value)
    return stream


def solution(mesh):
    placed = (
        P("seq", "head"),
        P(),
        P("head"),
        P(None, "head"),
        P(None, None, "head"),
        P("head", None),
        P(None, None, "head"),
        P(None, "seq", "head"),
        P(None, "head", "seq"),
        P(None, "seq", None),
    )
    return jax.shard_map(
        body, mesh=mesh, in_specs=placed, out_specs=P("seq", "head"), check_vma=False
    )
```

profile of v0, /device:TPU:2, one launch (start us, length us, event | category | flops | bytes accessed | tf_op | source)
XLA Modules:
  0.0 703.6 jit_solution(482095804169605450)
XLA Ops:
  8.4 32.0 %all_gather.37 = bf16[128,3072]{1,0:T(8,128)(2,1)S(1)} all-gather(bf16[128,384]{1,0:T(8,128)(2,1)} %param.12), channel_id=1, replica_groups=mesh['seq'=32,'head'=8] {'head'}, dimensions={1}, use_global_device_ids=true | all-gather | bytes 884736 | tf_op jit(solution)/shard_map/all_gather | solution.py:48
  44.8 3.5 collective-permute-start
  52.2 46.3 %reduce-scatter.13.cloned.1.call-done = bf16[384,128]{1,0:T(8,128)(2,1)} async-done(((bf16[3072,128]{1,0:T(8,128)(2,1)}), bf16[384,128]{1,0:T(8,128)(2,1)}) %reduce-scatter.13.cloned.1.call-update) | async-done | bytes 98320
  99.5 30.8 %all_gather.38 = bf16[128,3072]{1,0:T(8,128)(2,1)S(1)} all-gather(bf16[128,384]{1,0:T(8,128)(2,1)S(1)} %fusion.73), channel_id=1, replica_groups=mesh['seq'=32,'head'=8] {'head'}, dimensions={1}, use_global_device_ids=true | all-gather | bytes 884736 | tf_op jit(solution)/shard_map/all_gather | solution.py:48
  139.1 4.1 compare_and_fusion
  143.1 39.4 %all-gather.15.cloned.1.call-done = bf16[4096,128]{1,0:T(8,128)(2,1)} async-done(((bf16[128,128]{1,0:T(8,128)(2,1)}), bf16[4096,128]{1,0:T(8,128)(2,1)}) %all-gather.15.cloned.1.call-update) | async-done | bytes 1048592 | tf_op jit(solution)/shard_map/all_gather | solution.py:100
  182.5 2.7 gather_fusion
  185.2 49.4 %all-gather.17.cloned.1.call-done = bf16[4096,128]{1,0:T(8,128)(2,1)} async-done(((bf16[128,128]{1,0:T(8,128)(2,1)}), bf16[4096,128]{1,0:T(8,128)(2,1)}) %all-gather.17.cloned.1.call-update) | async-done | bytes 1048592 | tf_op jit(solution)/shard_map/all_gather | solution.py:99
  234.6 2.7 gather_fusion.1
  239.7 49.5 %all-gather.19.cloned.1.call-done = bf16[1,3072,384]{2,1,0:T(8,128)(2,1)} async-done(((bf16[1,96,384]{2,1,0:T(8,128)(2,1)}), bf16[1,3072,384]{2,1,0:T(8,128)(2,1)}) %all-gather.19.cloned.1.call-update) | async-done | bytes 2359312 | tf_op jit(solution)/shard_map/all_gather | solution.py:112
  295.2 48.1 %all-gather.21.cloned.1.call-done = bf16[1,384,3072]{1,2,0:T(8,128)(2,1)} async-done(((bf16[1,384,96]{1,2,0:T(8,128)(2,1)}), bf16[1,384,3072]{1,2,0:T(8,128)(2,1)}) %all-gather.21.cloned.1.call-update) | async-done | bytes 2359312 | tf_op jit(solution)/shard_map/all_gather | solution.py:144
  350.6 2.7 gather_fusion.5
  353.3 2.7 gather_fusion.2
  358.6 3.0 broadcast_select_fusion
  361.6 26.7 %reduce-scatter.15.cloned.1.call-done = bf16[384,128]{1,0:T(8,128)(2,1)} async-done(((bf16[3072,128]{1,0:T(8,128)(2,1)}), bf16[384,128]{1,0:T(8,128)(2,1)}) %reduce-scatter.15.cloned.1.call-update) | async-done | bytes 98320
  389.3 31.5 %all_gather.43 = bf16[128,3072]{1,0:T(8,128)(2,1)S(1)} all-gather(bf16[128,384]{1,0:T(8,128)(2,1)S(1)} %fusion.79), channel_id=1, replica_groups=mesh['seq'=32,'head'=8] {'head'}, dimensions={1}, use_global_device_ids=true | all-gather | bytes 884736 | tf_op jit(solution)/shard_map/all_gather | solution.py:48
  421.1 21.4 %all-gather.23.cloned.1.call-done = bf16[1,3072,384]{2,1,0:T(8,128)(2,1)} async-done(((bf16[1,96,384]{2,1,0:T(8,128)(2,1)}), bf16[1,3072,384]{2,1,0:T(8,128)(2,1)}) %all-gather.23.cloned.1.call-update) | async-done | bytes 2359312 | tf_op jit(solution)/shard_map/all_gather | solution.py:112
  448.5 48.3 %all-gather.25.cloned.1.call-done = bf16[1,384,3072]{1,2,0:T(8,128)(2,1)} async-done(((bf16[1,384,96]{1,2,0:T(8,128)(2,1)}), bf16[1,384,3072]{1,2,0:T(8,128)(2,1)}) %all-gather.25.cloned.1.call-update) | async-done | bytes 2359312 | tf_op jit(solution)/shard_map/all_gather | solution.py:144
  501.9 39.7 %reduce-scatter.17.cloned.1.call-done = bf16[384,128]{1,0:T(8,128)(2,1)} async-done(((bf16[3072,128]{1,0:T(8,128)(2,1)}), bf16[384,128]{1,0:T(8,128)(2,1)}) %reduce-scatter.17.cloned.1.call-update) | async-done | bytes 98320
  542.7 31.2 %all_gather.46 = bf16[128,3072]{1,0:T(8,128)(2,1)S(1)} all-gather(bf16[128,384]{1,0:T(8,128)(2,1)S(1)} %fusion.74), channel_id=1, replica_groups=mesh['seq'=32,'head'=8] {'head'}, dimensions={1}, use_global_device_ids=true | all-gather | bytes 884736 | tf_op jit(solution)/shard_map/all_gather | solution.py:48
  574.2 21.6 %all-gather.27.cloned.1.call-done = bf16[1,3072,384]{2,1,0:T(8,128)(2,1)} async-done(((bf16[1,96,384]{2,1,0:T(8,128)(2,1)}), bf16[1,3072,384]{2,1,0:T(8,128)(2,1)}) %all-gather.27.cloned.1.call-update) | async-done | bytes 2359312 | tf_op jit(solution)/shard_map/all_gather | solution.py:112
  595.8 2.9 fusion.49
  604.0 46.1 %all-gather.29.cloned.1.call-done = bf16[1,384,3072]{1,2,0:T(8,128)(2,1)} async-done(((bf16[1,384,96]{1,2,0:T(8,128)(2,1)}), bf16[1,384,3072]{1,2,0:T(8,128)(2,1)}) %all-gather.29.cloned.1.call-update) | async-done | bytes 2359312 | tf_op jit(solution)/shard_map/all_gather | solution.py:144
  653.9 41.1 %reduce-scatter.19.cloned.1.call-done = bf16[384,128]{1,0:T(8,128)(2,1)} async-done(((bf16[3072,128]{1,0:T(8,128)(2,1)}), bf16[384,128]{1,0:T(8,128)(2,1)}) %reduce-scatter.19.cloned.1.call-update) | async-done | bytes 98320
  (116 shorter events, 62.3 us)
Async XLA Ops:
  6.5 43.8 %copy-start = (bf16[384,3072]{1,0:T(8,128)(2,1)S(1)}, bf16[384,3072]{1,0:T(8,128)(2,1)}, u32[]{:S(2)}) copy-start(bf16[384,3072]{1,0:T(8,128)(2,1)} %param.17) | copy-start | bytes 7077892
  6.5 91.9 %reduce-scatter.13.cloned.1.call-start = ((), (), s32[]{:S(2)}) async-start(), calls=%async_computation.12 | async-start | bytes 884736
  6.5 37.8 %copy-start.7 = (bf16[2,3072,128]{2,1,0:T(8,128)(2,1)S(1)}, bf16[2,3072,128]{2,1,0:T(8,128)(2,1)}, u32[]{:S(2)}) copy-start(bf16[2,3072,128]{2,1,0:T(8,128)(2,1)} %param.16) | copy-start | bytes 4718596
  40.7 7.7 %copy-start.6 = (bf16[3072,384]{1,0:T(8,128)(2,1)S(1)}, bf16[3072,384]{1,0:T(8,128)(2,1)}, u32[]{:S(2)}) copy-start(bf16[3072,384]{1,0:T(8,128)(2,1)} %param.15) | copy-start | bytes 7077892
  42.5 6.8 collective-permute-start.1
  44.8 4.4 copy-start.8
  44.8 5.2 collective-permute-start
  50.3 49.2 %copy-start.1 = (bf16[128,384]{1,0:T(8,128)(2,1)S(1)}, bf16[128,384]{1,0:T(8,128)(2,1)}, u32[]{:S(2)}) copy-start(bf16[128,384]{1,0:T(8,128)(2,1)} %param.12) | copy-start | bytes 294916
  52.1 130.4 %all-gather.15.cloned.1.call-start = ((), (), s32[]{:S(2)}) async-start(), calls=%async_computation.4 | async-start | bytes 1081344 | tf_op jit(solution)/shard_map/all_gather | solution.py:100
  132.8 5.8 copy-start.5
  132.8 101.8 %all-gather.17.cloned.1.call-start = ((), (), s32[]{:S(2)}) async-start(), calls=%async_computation.5 | async-start | bytes 1081344 | tf_op jit(solution)/shard_map/all_gather | solution.py:99
  135.1 154.1 %all-gather.19.cloned.1.call-start = ((), (), s32[]{:S(2)}) async-start(), calls=%async_computation.6 | async-start | bytes 2433024 | tf_op jit(solution)/shard_map/all_gather | solution.py:112
  136.8 206.6 %all-gather.21.cloned.1.call-start = ((), (), s32[]{:S(2)}) async-start(), calls=%async_computation.7 | async-start | bytes 2433024 | tf_op jit(solution)/shard_map/all_gather | solution.py:144
  138.5 249.8 %reduce-scatter.15.cloned.1.call-start = ((), (), s32[]{:S(2)}) async-start(), calls=%async_computation.13 | async-start | bytes 884736
  293.4 1.0 copy-start.4
  347.2 95.3 %all-gather.23.cloned.1.call-start = ((), (), s32[]{:S(2)}) async-start(), calls=%async_computation.8 | async-start | bytes 2433024 | tf_op jit(solution)/shard_map/all_gather | solution.py:112
  347.9 148.9 %all-gather.25.cloned.1.call-start = ((), (), s32[]{:S(2)}) async-start(), calls=%async_computation.9 | async-start | bytes 2433024 | tf_op jit(solution)/shard_map/all_gather | solution.py:144
  348.7 193.0 %reduce-scatter.17.cloned.1.call-start = ((), (), s32[]{:S(2)}) async-start(), calls=%async_computation.14 | async-start | bytes 884736
  446.7 1.0 copy-start.3
  500.5 95.2 %all-gather.27.cloned.1.call-start = ((), (), s32[]{:S(2)}) async-start(), calls=%async_computation.10 | async-start | bytes 2433024 | tf_op jit(solution)/shard_map/all_gather | solution.py:112
  501.1 149.0 %all-gather.29.cloned.1.call-start = ((), (), s32[]{:S(2)}) async-start(), calls=%async_computation.11 | async-start | bytes 2433024 | tf_op jit(solution)/shard_map/all_gather | solution.py:144
  501.9 193.2 %reduce-scatter.19.cloned.1.call-start = ((), (), s32[]{:S(2)}) async-start(), calls=%async_computation.15 | async-start | bytes 884736
  601.5 1.0 copy-start.2
Sparse Core Ops, SparseCore 0:
  52.2 46.1 reduce-scatter.12
  132.9 49.5 all-gather.14
  185.1 49.4 all-gather.16
  237.0 52.1 all-gather.18
  291.6 51.7 all-gather.20
  347.3 40.9 reduce-scatter.14
  390.8 51.5 all-gather.22
  445.0 51.7 all-gather.24
  500.6 40.9 reduce-scatter.16
  544.0 51.7 all-gather.26
  598.3 51.7 all-gather.28
  654.0 40.9 reduce-scatter.18
where the time goes:
time: 705 us; the launch traced here: 704 us
  waiting for transfers between devices  481 us (68%)
  blocking collectives  126 us (18%)
  local copies, waits for them, and re-layouts  32.8 us (5%)
  matrix products  31.8 us (5%)
  between operations  14 us (2%)
  other arithmetic  12.8 us (2%)
    unnamed x16, waiting for transfers between devices  157 us
    all_gather x3, waiting for transfers between devices, body(): lax.all_gather(cross_output[section], 'seq', axis=1, tiled=True)  143 us
    all_gather x4, blocking collectives, normed_full(): lax.all_gather(stream.astype(jnp.float32).astype(jnp.bfloat16), 'head', a...  126 us
    all_gather x3, waiting for transfers between devices, body(): lax.all_gather(cross_query[section], 'seq', axis=0, tiled=True)  92.5 us
    all_gather x1, waiting for transfers between devices, body(): lax.all_gather(cached_key_rows, 'seq', axis=0, tiled=True)  49.4 us
    all_gather x1, waiting for transfers between devices, body(): lax.all_gather(cached_value_rows, 'seq', axis=0, tiled=True)  39.4 us
  transfers between devices with their start and end apart: 14, of which 13 were waited for; matrix products, arithmetic and copies ran while one was open for 8% of the time, Pallas kernels for 0%

commit v1 on v0

--- a/solution.py
+++ b/solution.py
@@ -9,6 +9,16 @@
 SECTIONS = 3
 EPSILON = 1e-06
 MASKED = -1e30
+
+
+def trails_match(matrix, where_dim=1):
+    nodes = []
+    for _ in range(lax.axis_size("seq")):
+        nodes.append(matrix)
+    return jnp.concatenate(
+        lax.all_to_all(jnp.stack(nodes), axis_name="seq", split_axis=0, concat_axis=0),
+        axis=where_dim,
+    )
 
 
 def passed_along(value, axis, steps):
@@ -140,9 +150,7 @@
         )
         context = context.astype(jnp.bfloat16).reshape(row_count, query_columns)
         partial_value = jnp.dot(
-            context,
-            lax.all_gather(cross_output[section], "seq", axis=1, tiled=True),
-            preferred_element_type=jnp.float32,
+            context, trails_match(cross_output[section]), preferred_element_type=jnp.float32
         )
         stream = add_branch(stream, partial_value)
     return stream

time: 705 us -> 647 us (0.918)
  waiting for transfers between devices: 481 us -> 372 us
  starting transfers between devices: 5.86 us -> 30.7 us
  blocking collectives: 126 us -> 143 us
    all_gather x3 -> x0, waiting for transfers between devices: 143 us -> none  [body(): lax.all_gather(cross_output[section], 'seq', axis=1, tiled=True)]
    unnamed x16 -> x13, waiting for transfers between devices: 157 us -> 184 us
    all_to_all x0 -> x3, starting transfers between devices: none -> 24.9 us  [trails_match(): lax.all_to_all(jnp.stack(nodes), axis_name='seq', split_axis=0, concat_ax...]
    all_gather x1, waiting for transfers between devices: 39.4 us -> 58 us  [body(): lax.all_gather(cached_value_rows, 'seq', axis=0, tiled=True)]
    all_gather x4, blocking collectives: 126 us -> 143 us  [normed_full(): lax.all_gather(stream.astype(jnp.float32).astype(jnp.bfloat16), 'head', a...]
    all_gather x3, waiting for transfers between devices: 92.5 us -> 78 us  [body(): lax.all_gather(cross_query[section], 'seq', axis=0, tiled=True)]
  transfers between devices with their start and end apart: 14 -> 14, of which waited for: 13 -> 10; matrix products, arithmetic and copies ran while one was open for 8% -> 10% of each run, Pallas kernels for 0% -> 0%
where the time goes in v1:
time: 647 us; the launch traced here: 646 us
  waiting for transfers between devices  372 us (57%)
  blocking collectives  143 us (22%)
  local copies, waits for them, and re-layouts  38 us (6%)
  matrix products  34.5 us (5%)
  starting transfers between devices  30.7 us (5%)
  between operations  13.7 us (2%)
  other arithmetic  13.3 us (2%)
    unnamed x13, waiting for transfers between devices  184 us
    all_gather x4, blocking collectives, normed_full(): lax.all_gather(stream.astype(jnp.float32).astype(jnp.bfloat16), 'head', a...  143 us
    all_gather x3, waiting for transfers between devices, body(): lax.all_gather(cross_query[section], 'seq', axis=0, tiled=True)  78 us
    all_gather x1, waiting for transfers between devices, body(): lax.all_gather(cached_value_rows, 'seq', axis=0, tiled=True)  58 us
    all_gather x1, waiting for transfers between devices, body(): lax.all_gather(cached_key_rows, 'seq', axis=0, tiled=True)  52 us
    all_to_all x3, starting transfers between devices, trails_match(): lax.all_to_all(jnp.stack(nodes), axis_name='seq', split_axis=0, concat_ax...  24.9 us
  transfers between devices with their start and end apart: 14, of which 10 were waited for; matrix products, arithmetic and copies ran while one was open for 10% of the time, Pallas kernels for 0%

profile of v1, /device:TPU:2, one launch (start us, length us, event | category | flops | bytes accessed | tf_op | source)
XLA Modules:
  0.0 645.6 jit_solution(13086367070947031729)
XLA Ops:
  7.8 32.2 %all_gather.28 = bf16[128,3072]{1,0:T(8,128)(2,1)S(1)} all-gather(bf16[128,384]{1,0:T(8,128)(2,1)} %param.12), channel_id=1, replica_groups=mesh['seq'=32,'head'=8] {'head'}, dimensions={1}, use_global_device_ids=true | all-gather | bytes 884736 | tf_op jit(solution)/shard_map/all_gather | solution.py:58
  44.4 3.5 collective-permute-start
  51.7 46.3 %reduce-scatter.13.cloned.1.call-done = bf16[384,128]{1,0:T(8,128)(2,1)} async-done(((bf16[3072,128]{1,0:T(8,128)(2,1)}), bf16[384,128]{1,0:T(8,128)(2,1)}) %reduce-scatter.13.cloned.1.call-update) | async-done | bytes 98320
  99.0 30.8 %all_gather.29 = bf16[128,3072]{1,0:T(8,128)(2,1)S(1)} all-gather(bf16[128,384]{1,0:T(8,128)(2,1)S(1)} %fusion.70), channel_id=1, replica_groups=mesh['seq'=32,'head'=8] {'head'}, dimensions={1}, use_global_device_ids=true | all-gather | bytes 884736 | tf_op jit(solution)/shard_map/all_gather | solution.py:58
  138.9 10.1 %all-to-all-start = ((bf16[32,384,96]{1,2,0:T(8,128)(2,1)}), bf16[32,384,96]{1,2,0:T(8,128)(2,1)}, u32[]{:S(2)}, u32[]{:S(2)}) async-start(bf16[32,384,96]{1,2,0:T(8,128)(2,1)} %stack.9), calls=%async_computation | async-start | bytes 4718592 | tf_op jit(solution)/shard_map/all_to_all | solution.py:19
  150.2 4.1 compare_and_fusion
  154.2 58.0 %all-gather.9.cloned.1.call-done = bf16[4096,128]{1,0:T(8,128)(2,1)} async-done(((bf16[128,128]{1,0:T(8,128)(2,1)}), bf16[4096,128]{1,0:T(8,128)(2,1)}) %all-gather.9.cloned.1.call-update) | async-done | bytes 1048592 | tf_op jit(solution)/shard_map/all_gather | solution.py:110
  212.2 2.7 gather_fusion
  214.9 52.0 %all-gather.11.cloned.1.call-done = bf16[4096,128]{1,0:T(8,128)(2,1)} async-done(((bf16[128,128]{1,0:T(8,128)(2,1)}), bf16[4096,128]{1,0:T(8,128)(2,1)}) %all-gather.11.cloned.1.call-update) | async-done | bytes 1048592 | tf_op jit(solution)/shard_map/all_gather | solution.py:109
  271.8 49.6 %all-gather.13.cloned.1.call-done = bf16[1,3072,384]{2,1,0:T(8,128)(2,1)} async-done(((bf16[1,96,384]{2,1,0:T(8,128)(2,1)}), bf16[1,3072,384]{2,1,0:T(8,128)(2,1)}) %all-gather.13.cloned.1.call-update) | async-done | bytes 2359312 | tf_op jit(solution)/shard_map/all_gather | solution.py:122
  321.4 2.9 fusion.40
  335.7 7.4 %all-to-all-start.1 = ((bf16[32,384,96]{1,2,0:T(8,128)(2,1)}), bf16[32,384,96]{1,2,0:T(8,128)(2,1)}, u32[]{:S(2)}, u32[]{:S(2)}) async-start(bf16[32,384,96]{1,2,0:T(8,128)(2,1)} %stack.10), calls=%async_computation.1 | async-start | bytes 4718592 | tf_op jit(solution)/shard_map/all_to_all | solution.py:19
  350.4 2.6 gather_fusion.3
  353.0 2.9 broadcast_select_fusion
  355.9 41.3 %reduce-scatter.15.cloned.1.call-done = bf16[384,128]{1,0:T(8,128)(2,1)} async-done(((bf16[3072,128]{1,0:T(8,128)(2,1)}), bf16[384,128]{1,0:T(8,128)(2,1)}) %reduce-scatter.15.cloned.1.call-update) | async-done | bytes 98320
  398.3 40.4 %all_gather.33 = bf16[128,3072]{1,0:T(8,128)(2,1)S(1)} all-gather(bf16[128,384]{1,0:T(8,128)(2,1)S(1)} %fusion.76), channel_id=1, replica_groups=mesh['seq'=32,'head'=8] {'head'}, dimensions={1}, use_global_device_ids=true | all-gather | bytes 884736 | tf_op jit(solution)/shard_map/all_gather | solution.py:58
  439.0 14.3 %all-gather.15.cloned.1.call-done = bf16[1,3072,384]{2,1,0:T(8,128)(2,1)} async-done(((bf16[1,96,384]{2,1,0:T(8,128)(2,1)}), bf16[1,3072,384]{2,1,0:T(8,128)(2,1)}) %all-gather.15.cloned.1.call-update) | async-done | bytes 2359312 | tf_op jit(solution)/shard_map/all_gather | solution.py:122
  453.3 2.9 fusion.43
  467.7 7.4 %all-to-all-start.2 = ((bf16[32,384,96]{1,2,0:T(8,128)(2,1)}), bf16[32,384,96]{1,2,0:T(8,128)(2,1)}, u32[]{:S(2)}, u32[]{:S(2)}) async-start(bf16[32,384,96]{1,2,0:T(8,128)(2,1)} %stack.11), calls=%async_computation.2 | async-start | bytes 4718592 | tf_op jit(solution)/shard_map/all_to_all | solution.py:19
  475.2 53.8 %reduce-scatter.17.cloned.1.call-done = bf16[384,128]{1,0:T(8,128)(2,1)} async-done(((bf16[3072,128]{1,0:T(8,128)(2,1)}), bf16[384,128]{1,0:T(8,128)(2,1)}) %reduce-scatter.17.cloned.1.call-update) | async-done | bytes 98320
  530.1 40.1 %all_gather.35 = bf16[128,3072]{1,0:T(8,128)(2,1)S(1)} all-gather(bf16[128,384]{1,0:T(8,128)(2,1)S(1)} %fusion.71), channel_id=1, replica_groups=mesh['seq'=32,'head'=8] {'head'}, dimensions={1}, use_global_device_ids=true | all-gather | bytes 884736 | tf_op jit(solution)/shard_map/all_gather | solution.py:58
  570.4 14.1 %all-gather.17.cloned.1.call-done = bf16[1,3072,384]{2,1,0:T(8,128)(2,1)} async-done(((bf16[1,96,384]{2,1,0:T(8,128)(2,1)}), bf16[1,3072,384]{2,1,0:T(8,128)(2,1)}) %all-gather.17.cloned.1.call-update) | async-done | bytes 2359312 | tf_op jit(solution)/shard_map/all_gather | solution.py:122
  584.5 2.9 fusion.46
  596.5 40.8 %reduce-scatter.19.cloned.1.call-done = bf16[384,128]{1,0:T(8,128)(2,1)} async-done(((bf16[3072,128]{1,0:T(8,128)(2,1)}), bf16[384,128]{1,0:T(8,128)(2,1)}) %reduce-scatter.19.cloned.1.call-update) | async-done | bytes 98320
  (128 shorter events, 68.8 us)
Async XLA Ops:
  6.5 43.3 %copy-start = (bf16[384,3072]{1,0:T(8,128)(2,1)S(1)}, bf16[384,3072]{1,0:T(8,128)(2,1)}, u32[]{:S(2)}) copy-start(bf16[384,3072]{1,0:T(8,128)(2,1)} %param.17) | copy-start | bytes 7077892
  6.5 91.4 %reduce-scatter.13.cloned.1.call-start = ((), (), s32[]{:S(2)}) async-start(), calls=%async_computation.12 | async-start | bytes 884736
  6.5 37.4 %copy-start.11 = (bf16[2,3072,128]{2,1,0:T(8,128)(2,1)S(1)}, bf16[2,3072,128]{2,1,0:T(8,128)(2,1)}, u32[]{:S(2)}) copy-start(bf16[2,3072,128]{2,1,0:T(8,128)(2,1)} %param.16) | copy-start | bytes 4718596
  40.3 7.7 %copy-start.10 = (bf16[3072,384]{1,0:T(8,128)(2,1)S(1)}, bf16[3072,384]{1,0:T(8,128)(2,1)}, u32[]{:S(2)}) copy-start(bf16[3072,384]{1,0:T(8,128)(2,1)} %param.15) | copy-start | bytes 7077892
  42.0 6.8 %collective-permute-start.1 = (bf16[128,128]{1,0:T(8,128)(2,1)S(1)}, bf16[128,128]{1,0:T(8,128)(2,1)S(1)}, u32[]{:S(2)}, u32[]{:S(2)}) collective-permute-start(bf16[128,128]{1,0:T(8,128)(2,1)S(1)} %convolution_convert_fusion.8), channel_id=1, source_target_pairs={{0,8},{8,16},{16,24},{24,32},{32,40},{40,48},{48,56},{56,64},{64,7... | collective-permute-start | bytes 98312 | tf_op jit(solution)/shard_map/ppermute | solution.py:27
  44.4 5.2 collective-permute-start
  49.9 49.1 %copy-start.1 = (bf16[128,384]{1,0:T(8,128)(2,1)S(1)}, bf16[128,384]{1,0:T(8,128)(2,1)}, u32[]{:S(2)}) copy-start(bf16[128,384]{1,0:T(8,128)(2,1)} %param.12) | copy-start | bytes 294916
  51.7 160.6 %all-gather.9.cloned.1.call-start = ((), (), s32[]{:S(2)}) async-start(), calls=%async_computation.7 | async-start | bytes 1081344 | tf_op jit(solution)/shard_map/all_gather | solution.py:110
  132.3 134.5 %all-gather.11.cloned.1.call-start = ((), (), s32[]{:S(2)}) async-start(), calls=%async_computation.8 | async-start | bytes 1081344 | tf_op jit(solution)/shard_map/all_gather | solution.py:109
  134.6 186.8 %all-gather.13.cloned.1.call-start = ((), (), s32[]{:S(2)}) async-start(), calls=%async_computation.9 | async-start | bytes 2433024 | tf_op jit(solution)/shard_map/all_gather | solution.py:122
  138.9 10.2 %copy-start.5 = (s32[3,1,16]{2,1,0:T(1,128)S(1)}, s32[3,1,16]{2,1,0:T(1,128)}, u32[]{:S(2)}) copy-start(s32[3,1,16]{2,1,0:T(1,128)} %param.21) | copy-start | bytes 580
  138.9 190.7 %all-to-all-start = ((bf16[32,384,96]{1,2,0:T(8,128)(2,1)}), bf16[32,384,96]{1,2,0:T(8,128)(2,1)}, u32[]{:S(2)}, u32[]{:S(2)}) async-start(bf16[32,384,96]{1,2,0:T(8,128)(2,1)} %stack.9), calls=%async_computation | async-start | bytes 4718592 | tf_op jit(solution)/shard_map/all_to_all | solution.py:19
  149.0 248.2 %reduce-scatter.15.cloned.1.call-start = ((), (), s32[]{:S(2)}) async-start(), calls=%async_computation.13 | async-start | bytes 884736
  154.2 167.2 %copy-start.14 = (f32[128]{0:T(128)S(1)}, f32[128]{0:T(128)}, u32[]{:S(2)}) copy-start(f32[128]{0:T(128)} %copy-done.13) | copy-start | bytes 1540
  333.5 119.8 %all-gather.15.cloned.1.call-start = ((), (), s32[]{:S(2)}) async-start(), calls=%async_computation.10 | async-start | bytes 2433024 | tf_op jit(solution)/shard_map/all_gather | solution.py:122
  335.7 7.5 %copy-start.9 = (s32[16]{0:T(128)S(1)}, s32[16]{0:T(128)}, u32[]{:S(2)}) copy-start(s32[16]{0:T(128)} %get-tuple-element.32) | copy-start | bytes 196
  335.7 7.5 %copy-start.8 = (s32[16]{0:T(128)S(1)}, s32[16]{0:T(128)}, u32[]{:S(2)}) copy-start(s32[16]{0:T(128)} %get-tuple-element.30) | copy-start | bytes 196
  335.7 125.8 %all-to-all-start.1 = ((bf16[32,384,96]{1,2,0:T(8,128)(2,1)}), bf16[32,384,96]{1,2,0:T(8,128)(2,1)}, u32[]{:S(2)}, u32[]{:S(2)}) async-start(bf16[32,384,96]{1,2,0:T(8,128)(2,1)} %stack.10), calls=%async_computation.1 | async-start | bytes 4718592 | tf_op jit(solution)/shard_map/all_to_all | solution.py:19
  343.1 9.9 %copy-start.6 = (pred[16]{0:T(512)(128)(4,1)S(1)}, pred[16]{0:T(512)(128)(4,1)}, u32[]{:S(2)}) copy-start(pred[16]{0:T(512)(128)(4,1)} %get-tuple-element.29) | copy-start | bytes 52
  343.1 9.9 %copy-start.7 = (pred[16]{0:T(512)(128)(4,1)S(1)}, pred[16]{0:T(512)(128)(4,1)}, u32[]{:S(2)}) copy-start(pred[16]{0:T(512)(128)(4,1)} %get-tuple-element.31) | copy-start | bytes 52
  343.1 185.9 %reduce-scatter.17.cloned.1.call-start = ((), (), s32[]{:S(2)}) async-start(), calls=%async_computation.14 | async-start | bytes 884736
  465.3 119.2 %all-gather.17.cloned.1.call-start = ((), (), s32[]{:S(2)}) async-start(), calls=%async_computation.11 | async-start | bytes 2433024 | tf_op jit(solution)/shard_map/all_gather | solution.py:122
  467.7 125.0 %all-to-all-start.2 = ((bf16[32,384,96]{1,2,0:T(8,128)(2,1)}), bf16[32,384,96]{1,2,0:T(8,128)(2,1)}, u32[]{:S(2)}, u32[]{:S(2)}) async-start(bf16[32,384,96]{1,2,0:T(8,128)(2,1)} %stack.11), calls=%async_computation.2 | async-start | bytes 4718592 | tf_op jit(solution)/shard_map/all_to_all | solution.py:19
  475.1 162.2 %reduce-scatter.19.cloned.1.call-start = ((), (), s32[]{:S(2)}) async-start(), calls=%async_computation.15 | async-start | bytes 884736
  (5 other events, 12.0 us)
Sparse Core Ops, SparseCore 0:
  51.8 46.1 reduce-scatter.12
  132.5 79.7 all-gather.8
  214.8 51.9 all-gather.10
  269.2 52.1 all-gather.12
  333.6 63.6 reduce-scatter.14
  399.7 53.5 all-gather.14
  465.4 63.5 reduce-scatter.16
  531.6 52.9 all-gather.16
  596.7 40.6 reduce-scatter.18
